TPU v7x, 32 devices: a whole 2x2x4 slice. The times are simulated.
32 devices in a mesh: dp: 4 (over y, x), segment: 2 (over core), band: 4 (over z).
Axes of the slice: x: 2, y: 2, z: 4, core: 2. Of those that a mesh axis runs over, the one named last changes fastest.
Arguments:
- fields: bfloat16 [4, 2, 32, 16, 512], P('dp', None, 'band'), may hold values from -6 to 6
- cell_mask: int32 [4, 2, 32, 16], P('dp', None, 'band'), may hold values 0 or 1
- merge_weight: bfloat16 [2, 1024, 512], P('segment', 'dp'), may hold values from -0.1875 to 0.1875
- qkv_weight: bfloat16 [2, 512, 1536], P('segment', 'dp')
- out_weight: bfloat16 [2, 512, 512], P('segment', 'dp'), may hold values from -1 to 1
- norm_gain: bfloat16 [2, 512], P('segment', 'dp'), may hold values from 0.099609375 to 1.8984375
- out_cotangent: bfloat16 [4, 2, 32, 16, 512], P('dp', None, 'band'), may hold values from -6 to 6
Outputs:
- section_out: bfloat16 [2, 4, 2, 32, 16, 512], P('segment', 'dp', None, 'band')
- merge_grad: float32 [2, 1024, 512], P('segment', 'dp')
- qkv_grad: float32 [2, 512, 1536], P('segment', 'dp')
- out_grad: float32 [2, 512, 512], P('segment', 'dp')
- gain_grad: float32 [2, 512], P('segment', 'dp')
Inputs may be any that keep to these rules, and one draw needn't show every extreme that they name: `cell_mask`: 1 marks a cell whose keys may be attended.
All inputs are finite; a program needn't handle non-finite values. No bound on the sum of `cell_mask` on one device may be relied on, other than what follows from the above.
Results may differ from a plain program's by a relative error of at most 0.03.
Values may be sent and summed in bfloat16 or wider, within the bound.
No kernel may reach another device: no remote copies, remote signals or barrier semaphores. Data moves between devices by JAX's collectives and lax.ppermute only.
A program may use at most 128 MiB of HBM per device.

v0:
```python
import jax
import jax.numpy as jnp
from jax import lax
from jax.sharding import PartitionSpec as P

HEADS = 8
WH = 8
WW = 16
SH = 4
SW = 8
EPSILON = 1e-05
MASKED = -1e30


def padded(shard, sides, width):
    for axis, dim in sides:
        size, length = (lax.axis_size(axis), shard.shape[dim])
        up = [(i, (i + 1) % size) for i in range(size - 1)]
        down = [(j, i) for i, j in up]
        last = lax.slice_in_dim(shard, length - width, length, axis=dim)
        first = lax.slice_in_dim(shard, 0, width, axis=dim)
        before = lax.ppermute(last, axis, up)
        after = lax.ppermute(first, axis, down)
        shard = jnp.concatenate([before, shard, after], axis=dim)
    return shard


def normalize(update):
    average = jnp.mean(update, axis=-1, keepdims=True)
    centered = update - average
    spread = jnp.mean(centered * centered, axis=-1, keepdims=True)
    inverse = lax.rsqrt(spread + EPSILON)
    return (centered * inverse, inverse)


def window_pattern(lon_count):
    query_index = jnp.arange(WH * lon_count, dtype=jnp.int32)
    key_index = jnp.arange(2 * WH * lon_count, dtype=jnp.int32)
    query_row = query_index // lon_count
    query_col = query_index % lon_count
    key_row = key_index // lon_count
    key_col = key_index % lon_count
    lat_same = ((query_row + SH) // WH)[:, None] == (key_row // WH)[None, :]
    lon_same = ((query_col + SW) // WW)[:, None] == ((key_col + SW) // WW)[None, :]
    self_key = ((query_row + SH)[:, None] == key_row[None, :]) & (
        query_col[:, None] == key_col[None, :]
    )
    return (lat_same & lon_same, self_key)


def attend(queries, keyvals, usable):
    row_count, lon_count, feature = queries.shape
    blocks = row_count // WH
    head_dim = feature // HEADS
    query_blocks = queries.reshape(blocks, WH * lon_count, HEADS, head_dim)
    kv_blocks = keyvals.reshape(blocks + 1, WH * lon_count, 2, HEADS, head_dim)
    key_pairs = jnp.concatenate([kv_blocks[:-1], kv_blocks[1:]], axis=1)
    use_blocks = usable.reshape(blocks + 1, WH * lon_count)
    use_pairs = jnp.concatenate([use_blocks[:-1], use_blocks[1:]], axis=1)
    inside, self_key = window_pattern(lon_count)
    allowed = inside[None] & (use_pairs[:, None, :] | self_key[None])
    scores = jnp.einsum(
        "nqhd,nkhd->nhqk", query_blocks, key_pairs[:, :, 0], preferred_element_type=jnp.float32
    ) * head_dim ** (-0.5)
    scores = jnp.where(allowed[:, None], scores, MASKED)
    highest = jnp.max(scores, axis=-1, keepdims=True)
    weights = jnp.exp(scores - highest)
    attn_prob = (weights / jnp.sum(weights, axis=-1, keepdims=True)).astype(jnp.bfloat16)
    mixture = jnp.einsum(
        "nhqk,nkhd->nqhd", attn_prob, key_pairs[:, :, 1], preferred_element_type=jnp.float32
    )
    return mixture.reshape(row_count, lon_count, feature).astype(jnp.bfloat16)


def guarded(active, function, operands):

    def skipped(values):
        return jax.tree.map(jnp.zeros_like, function(values))

    return lax.cond(active, function, skipped, operands)


def project(joined, merge_full, qkv_full, gain_full):
    update = jnp.einsum("rwj,jd->rwd", joined, merge_full, preferred_element_type=jnp.float32)
    normed, inverse = normalize(update)
    hidden = (normed * gain_full.astype(jnp.float32)).astype(jnp.bfloat16)
    projected = jnp.einsum("rwd,de->rwe", hidden, qkv_full, preferred_element_type=jnp.float32)
    feature = update.shape[-1]
    queries = projected[..., :feature].astype(jnp.bfloat16)
    keyvals = projected[..., feature:].astype(jnp.bfloat16)
    return (update, normed, inverse, hidden, queries, keyvals)


def section_forward(active, joined, usable, merge_full, qkv_full, gain_full, out_full):
    update, normed, inverse, hidden, queries, own_keys = guarded(
        active, lambda rows_own: project(rows_own, merge_full, qkv_full, gain_full), joined
    )
    keyvals = padded(own_keys, (("band", 0),), SH)

    def finish(operands):
        update_in, query_in, keyval_in, usable_in = operands
        mixture = attend(query_in, keyval_in, usable_in)
        result = (
            update_in
            + jnp.einsum("rwd,de->rwe", mixture, out_full, preferred_element_type=jnp.float32)
        ).astype(jnp.bfloat16)
        return (mixture, result)

    mixture, result = guarded(active, finish, (update, queries, keyvals, usable))
    return (result, (joined, normed, inverse, hidden, queries, keyvals, mixture))


def attend_back(out_full, operands):
    grad_out, queries, keyvals, mixture, usable = operands
    grad_mixture = jnp.einsum(
        "rwe,de->rwd", grad_out, out_full, preferred_element_type=jnp.float32
    ).astype(jnp.bfloat16)
    unused, pull_back = jax.vjp(
        lambda query_in, keyval_in: attend(query_in, keyval_in, usable), queries, keyvals
    )
    grad_query, grad_keyval = pull_back(grad_mixture)
    grad_outw = jnp.einsum("rwd,rwe->de", mixture, grad_out, preferred_element_type=jnp.float32)
    return (grad_query, grad_keyval, grad_outw)


def fold_rims(grad_keyval, row_count):
    rim_rows = jnp.concatenate([grad_keyval[:SH], grad_keyval[SH + row_count :]], axis=0)
    returned = padded(rim_rows, (("band", 0),), SH)
    own_part = grad_keyval[SH : SH + row_count].astype(jnp.float32)
    return jnp.concatenate(
        [
            own_part[:SH] + returned[:SH].astype(jnp.float32),
            own_part[SH : row_count - SH],
            own_part[row_count - SH :] + returned[3 * SH :].astype(jnp.float32),
        ],
        axis=0,
    ).astype(jnp.bfloat16)


def back_core(qkv_full, gain_full, grad_query, grad_keyown, grad_out, normed, inverse):
    grad_proj = jnp.concatenate([grad_query, grad_keyown], axis=-1)
    grad_hidden = jnp.einsum("rwe,de->rwd", grad_proj, qkv_full, preferred_element_type=jnp.float32)
    grad_normed = grad_hidden * gain_full.astype(jnp.float32)
    grad_update = (
        grad_out.astype(jnp.float32)
        + inverse
        * (
            grad_normed
            - jnp.mean(grad_normed, axis=-1, keepdims=True)
            - normed * jnp.mean(grad_normed * normed, axis=-1, keepdims=True)
        )
    ).astype(jnp.bfloat16)
    return (grad_proj, grad_hidden, grad_update)


def body(fields, cell_mask, merge_weight, qkv_weight, out_weight, norm_gain, out_cotangent):
    merge_rows, qkv_rows, out_rows, gain_rows = (
        lax.all_gather(merge_weight, "dp", axis=1, tiled=True),
        lax.all_gather(qkv_weight, "dp", axis=1, tiled=True),
        lax.all_gather(out_weight, "dp", axis=1, tiled=True),
        lax.all_gather(norm_gain, "dp", axis=1, tiled=True),
    )
    merge_full = merge_rows[0]
    qkv_full = qkv_rows[0]
    inputs = fields[0]
    cotangent = out_cotangent[0]
    micro_count, row_count, lon_count, feature = inputs.shape
    mask_ext = padded(cell_mask[0], (("band", 1),), SH)
    usable_ext = mask_ext == 1
    section_count = lax.axis_size("segment")
    half_count = section_count // 2
    section_rank = lax.axis_index("segment")
    merge_all, qkv_all, out_all, gain_all = (
        lax.all_gather(merge_rows, "segment", axis=0, tiled=True),
        lax.all_gather(qkv_rows, "segment", axis=0, tiled=True),
        lax.all_gather(out_rows, "segment", axis=0, tiled=True),
        lax.all_gather(gain_rows, "segment", axis=0, tiled=True),
    )
    local_count = micro_count // section_count
    always = jnp.array(True)
    shipped = [[] for index in range(section_count)]
    pick = section_rank * local_count + 0
    inputs_now = lax.dynamic_index_in_dim(inputs, pick, 0, keepdims=False)
    cotangent_now = lax.dynamic_index_in_dim(cotangent, pick, 0, keepdims=False)
    usable_now = lax.dynamic_index_in_dim(usable_ext, pick, 0, keepdims=False)
    outputs = []
    records = []
    for index in range(section_count):
        chain_in = inputs_now if index == 0 else outputs[index - 1]
        side_in = inputs_now if index < half_count else outputs[section_count - 1 - index]
        joined = jnp.concatenate([chain_in, side_in], axis=-1)
        result, record = section_forward(
            always,
            joined,
            usable_now,
            merge_all[index],
            qkv_all[index],
            gain_all[index],
            out_all[index],
        )
        outputs.append(result)
        records.append(record)
    flows = [None] * section_count
    for index in range(section_count - 1, -1, -1):
        grad_out = (
            cotangent_now if index == section_count - 1 else flows[index].astype(jnp.bfloat16)
        )
        joined, normed, inverse, hidden, queries, keyvals, mixture = records[index]
        grad_query, grad_keyval, unused = attend_back(
            out_all[index], (grad_out, queries, keyvals, mixture, usable_now)
        )
        grad_keyown = fold_rims(grad_keyval, row_count)
        grad_proj, unused, grad_update = back_core(
            qkv_all[index], gain_all[index], grad_query, grad_keyown, grad_out, normed, inverse
        )
        grad_joined = jnp.einsum(
            "rwd,jd->rwj", grad_update, merge_all[index], preferred_element_type=jnp.float32
        )
        grad_chain = grad_joined[..., :feature].astype(jnp.bfloat16).astype(jnp.float32)
        grad_side = grad_joined[..., feature:].astype(jnp.bfloat16).astype(jnp.float32)
        if index > 0:
            flows[index - 1] = grad_chain
        if index >= half_count:
            target = section_count - 1 - index
            flows[target] = flows[target] + grad_side
        shipped[index].append(
            (outputs[index], joined, grad_update, hidden, grad_proj, mixture, grad_out)
        )
    packed = tuple(
        (
            jnp.stack([jnp.stack([shipped[index][0][field]]) for index in range(section_count)])
            for field in range(7)
        )
    )
    home = (
        lax.all_to_all(packed[0], "segment", split_axis=0, concat_axis=1, tiled=True),
        lax.all_to_all(packed[1], "segment", split_axis=0, concat_axis=1, tiled=True),
        lax.all_to_all(packed[2], "segment", split_axis=0, concat_axis=1, tiled=True),
        lax.all_to_all(packed[3], "segment", split_axis=0, concat_axis=1, tiled=True),
        lax.all_to_all(packed[4], "segment", split_axis=0, concat_axis=1, tiled=True),
        lax.all_to_all(packed[5], "segment", split_axis=0, concat_axis=1, tiled=True),
        lax.all_to_all(packed[6], "segment", split_axis=0, concat_axis=1, tiled=True),
    )
    joined_all, grad_update_all, hidden_all, grad_proj_all, mixture_all, grad_out_all = [
        part[0] for part in home[1:]
    ]
    grad_merge = jnp.einsum(
        "mrwj,mrwd->jd", joined_all, grad_update_all, preferred_element_type=jnp.float32
    )
    grad_qkv = jnp.einsum(
        "mrwd,mrwe->de", hidden_all, grad_proj_all, preferred_element_type=jnp.float32
    )
    grad_outw = jnp.einsum(
        "mrwd,mrwe->de", mixture_all, grad_out_all, preferred_element_type=jnp.float32
    )
    update_all = jnp.einsum(
        "mrwj,jd->mrwd", joined_all, merge_full, preferred_element_type=jnp.float32
    )
    normed_all, unused = normalize(update_all)
    grad_hidden_all = jnp.einsum(
        "mrwe,de->mrwd", grad_proj_all, qkv_full, preferred_element_type=jnp.float32
    )
    grad_gain = jnp.sum(grad_hidden_all * normed_all, axis=(0, 1, 2))
    grad_sums = (grad_merge, grad_qkv, grad_outw, grad_gain)
    section_home = home[0][None]
    merge_part_sum, qkv_part_sum, out_part_sum, gain_part_sum = (
        lax.psum_scatter(
            grad_sums[0][None].astype(jnp.bfloat16), "dp", scatter_dimension=1, tiled=True
        ).astype(jnp.float32),
        lax.psum_scatter(
            grad_sums[1][None].astype(jnp.bfloat16), "dp", scatter_dimension=1, tiled=True
        ).astype(jnp.float32),
        lax.psum_scatter(
            grad_sums[2][None].astype(jnp.bfloat16), "dp", scatter_dimension=1, tiled=True
        ).astype(jnp.float32),
        lax.psum_scatter(
            grad_sums[3][None].astype(jnp.bfloat16), "dp", scatter_dimension=1, tiled=True
        ).astype(jnp.float32),
    )
    merge_grad, qkv_grad, out_grad, gain_grad = (
        lax.psum(merge_part_sum.astype(jnp.bfloat16), "band").astype(jnp.float32),
        lax.psum(qkv_part_sum.astype(jnp.bfloat16), "band").astype(jnp.float32),
        lax.psum(out_part_sum.astype(jnp.bfloat16), "band").astype(jnp.float32),
        lax.psum(gain_part_sum.astype(jnp.bfloat16), "band").astype(jnp.float32),
    )
    return (section_home, merge_grad, qkv_grad, out_grad, gain_grad)


def solution(mesh):
    return jax.shard_map(
        body,
        mesh=mesh,
        in_specs=(
            P("dp", None, "band", None, None),
            P("dp", None, "band", None),
            P("segment", "dp", None),
            P("segment", "dp", None),
            P("segment", "dp", None),
            P("segment", "dp"),
            P("dp", None, "band", None, None),
        ),
        out_specs=(
            P("segment", "dp", None, "band", None, None),
            P("segment", "dp", None),
            P("segment", "dp", None),
            P("segment", "dp", None),
            P("segment", "dp"),
        ),
        check_vma=False,
    )
```

profile of v0, /device:TPU:0, one launch (start us, length us, event | category | flops | bytes accessed | tf_op | source)
XLA Modules:
  0.0 377.2 jit_solution(2174182986141230632)
XLA Ops:
  8.8 30.4 %all-gather.7.cloned.1.call-done = bf16[1,1024,512]{2,1,0:T(8,128)(2,1)} async-done(((bf16[1,256,512]{2,1,0:T(8,128)(2,1)}), bf16[1,1024,512]{2,1,0:T(8,128)(2,1)}) %all-gather.7.cloned.1.call-update) | async-done | bytes 1048592 | tf_op jit(solution)/shard_map/all_gather | solution.py:158
  39.2 32.6 %all-gather.11.cloned.1.call-done = bf16[1,512,1536]{2,1,0:T(8,128)(2,1)} async-done(((bf16[1,128,1536]{2,1,0:T(8,128)(2,1)}), bf16[1,512,1536]{2,1,0:T(8,128)(2,1)}) %all-gather.11.cloned.1.call-update) | async-done | bytes 1572880 | tf_op jit(solution)/shard_map/all_gather | solution.py:159
  73.2 4.5 %collective-permute-start.2 = (s32[2,4,16]{2,1,0:T(4,128)S(1)}, s32[2,4,16]{2,1,0:T(4,128)S(1)}, u32[]{:S(2)}, u32[]{:S(2)}) collective-permute-start(s32[2,4,16]{2,1,0:T(4,128)S(1)} %get-tuple-element.47), channel_id=1, source_target_pairs={{0,1},{1,2},{2,3},{4,5},{5,6},{6,7},{8,9},{9,10},{10,11},{12,13},{... | collective-permute-start | bytes 1544 | tf_op jit(solution)/shard_map/ppermute | solution.py:22
  77.8 10.6 %all_gather.30 = bf16[1,512,512]{2,1,0:T(8,128)(2,1)} all-gather(bf16[1,128,512]{2,1,0:T(8,128)(2,1)S(1)} %copy-done.33), channel_id=1, replica_groups=mesh['dp'=4,'segment'=2,'band'=4] {'dp'}, dimensions={1}, use_global_device_ids=true | all-gather | bytes 655360 | tf_op jit(solution)/shard_map/all_gather | solution.py:160
  88.5 7.1 %all_gather.26 = bf16[1,512]{1,0:T(2,128)(2,1)S(1)} all-gather(bf16[1,128]{1,0:T(2,128)(2,1)S(1)} %copy-done.44), channel_id=1, replica_groups=mesh['dp'=4,'segment'=2,'band'=4] {'dp'}, dimensions={1}, use_global_device_ids=true | all-gather | bytes 1280 | tf_op jit(solution)/shard_map/all_gather | solution.py:161
  95.6 1.8 all-gather
  100.4 1.8 convolution_convert_fusion.1
  102.3 3.4 collective-permute-start
  107.0 3.3 all-gather.15.cloned.1.call-done
  125.8 3.4 collective-permute-start.4
  132.7 3.8 %collective-permute-done.5 = bf16[4,16,1024]{2,1,0:T(8,128)(2,1)S(1)} collective-permute-done((bf16[4,16,1024]{2,1,0:T(8,128)(2,1)S(1)}, bf16[4,16,1024]{2,1,0:T(8,128)(2,1)S(1)}, u32[]{:S(2)}, u32[]{:S(2)}) %collective-permute-start.5) | collective-permute-done | bytes 131104 | tf_op jit(solution)/shard_map/ppermute | solution.py:23
  149.3 4.1 %all-to-all-start.5 = ((bf16[2,1,8,16,512]{4,3,2,1,0:T(8,128)(2,1)}), bf16[2,1,8,16,512]{4,3,2,1,0:T(8,128)(2,1)}, u32[]{:S(2)}, u32[]{:S(2)}) async-start(bf16[2,1,8,16,512]{4,3,2,1,0:T(8,128)(2,1)} %pad_maximum_fusion.13), calls=%async_computation.7 | async-start | bytes 524288 | tf_op jit(solution)/shard_map/all_to_all | solution.py:241
  161.1 3.4 collective-permute-start.6
  167.8 4.1 %collective-permute-done.7 = bf16[4,16,1024]{2,1,0:T(8,128)(2,1)S(1)} collective-permute-done((bf16[4,16,1024]{2,1,0:T(8,128)(2,1)S(1)}, bf16[4,16,1024]{2,1,0:T(8,128)(2,1)S(1)}, u32[]{:S(2)}, u32[]{:S(2)}) %collective-permute-start.7) | collective-permute-done | bytes 131104 | tf_op jit(solution)/shard_map/ppermute | solution.py:23
  172.0 2.3 fusion.126
  183.2 3.4 collective-permute-start.8
  189.1 4.4 %collective-permute-done.9 = bf16[4,16,1024]{2,1,0:T(8,128)(2,1)S(1)} collective-permute-done((bf16[4,16,1024]{2,1,0:T(8,128)(2,1)S(1)}, bf16[4,16,1024]{2,1,0:T(8,128)(2,1)S(1)}, u32[]{:S(2)}, u32[]{:S(2)}) %collective-permute-start.9) | collective-permute-done | bytes 131104 | tf_op jit(solution)/shard_map/ppermute | solution.py:23
  193.5 2.2 fusion.125
  196.0 3.9 %all_to_all.28 = bf16[2,1,8,16,512]{4,3,2,1,0:T(8,128)(2,1)S(1)} all-to-all(bf16[2,1,8,16,512]{4,3,2,1,0:T(8,128)(2,1)S(1)} %pad_maximum_fusion.14), channel_id=1, replica_groups=mesh['dp'=4,'segment'=2,'band'=4] {'segment'}, dimensions={0} | all-to-all | bytes 524288 | tf_op jit(solution)/shard_map/all_to_all | solution.py:242
  199.9 2.1 fusion.10
  203.0 3.5 all-to-all-start.1
  208.2 3.9 %all_to_all.29 = bf16[2,1,8,16,512]{4,3,2,1,0:T(8,128)(2,1)S(1)} all-to-all(bf16[2,1,8,16,512]{4,3,2,1,0:T(8,128)(2,1)S(1)} %pad_maximum_fusion.11), channel_id=1, replica_groups=mesh['dp'=4,'segment'=2,'band'=4] {'segment'}, dimensions={0} | all-to-all | bytes 524288 | tf_op jit(solution)/shard_map/all_to_all | solution.py:238
  214.4 3.4 all-to-all-start.3
  220.1 4.4 %all_to_all.30 = bf16[2,1,8,16,1536]{4,3,2,1,0:T(8,128)(2,1)S(1)} all-to-all(bf16[2,1,8,16,1536]{4,3,2,1,0:T(8,128)(2,1)S(1)} %pad_maximum_fusion), channel_id=1, replica_groups=mesh['dp'=4,'segment'=2,'band'=4] {'segment'}, dimensions={0} | all-to-all | bytes 1572864 | tf_op jit(solution)/shard_map/all_to_all | solution.py:240
  224.4 2.8 fusion.1
  230.3 26.1 %reduce-scatter.7.cloned.1.call-done = bf16[1,256,512]{2,1,0:T(8,128)(2,1)} async-done(((bf16[1,1024,512]{2,1,0:T(8,128)(2,1)}), bf16[1,256,512]{2,1,0:T(8,128)(2,1)}) %reduce-scatter.7.cloned.1.call-update) | async-done | bytes 262160 | tf_op jit(solution)/shard_map/reduce_scatter | solution.py:267
  256.3 34.2 %reduce-scatter.9.cloned.1.call-done = bf16[1,128,1536]{2,1,0:T(8,128)(2,1)} async-done(((bf16[1,512,1536]{2,1,0:T(8,128)(2,1)}), bf16[1,128,1536]{2,1,0:T(8,128)(2,1)}) %reduce-scatter.9.cloned.1.call-update) | async-done | bytes 393232 | tf_op jit(solution)/shard_map/reduce_scatter | solution.py:270
  291.0 3.9 %all_to_all.31 = bf16[2,1,8,16,512]{4,3,2,1,0:T(8,128)(2,1)S(1)} all-to-all(bf16[2,1,8,16,512]{4,3,2,1,0:T(8,128)(2,1)S(1)} %pad_maximum_fusion.10), channel_id=1, replica_groups=mesh['dp'=4,'segment'=2,'band'=4] {'segment'}, dimensions={0} | all-to-all | bytes 524288 | tf_op jit(solution)/shard_map/all_to_all | solution.py:236
  295.0 23.0 %reduce-scatter.13.cloned.1.call-done = bf16[128,1]{1,0:T(8,128)(2,1)} async-done(((bf16[512,1]{1,0:T(8,128)(2,1)}), bf16[128,1]{1,0:T(8,128)(2,1)}) %reduce-scatter.13.cloned.1.call-update) | async-done | bytes 272
  318.8 11.7 %psum.31 = bf16[1,128]{1,0:T(2,128)(2,1)S(1)} all-reduce(bf16[1,128]{1,0:T(2,128)(2,1)S(1)} %copy.77), channel_id=1, replica_groups=mesh['dp'=4,'segment'=2,'band'=4] {'band'}, use_global_device_ids=true, to_apply=%region_28.29 | all-reduce | flops 128 | bytes 512 | tf_op jit(solution)/shard_map/psum | solution.py:284
  331.0 33.2 %all-reduce.11.cloned.1.call-done = (bf16[1,256,512]{2,1,0:T(8,128)(2,1)}, bf16[1,128,1536]{2,1,0:T(8,128)(2,1)}, bf16[1,128,512]{2,1,0:T(8,128)(2,1)}) async-done(((bf16[1,256,512]{2,1,0:T(8,128)(2,1)}, bf16[1,128,1536]{2,1,0:T(8,128)(2,1)}, bf16[1,128,512]{2,1,0:T(8,128)(2,1)}), (bf16[1,256,512]{2,1,0:T(8,128)(2,1)}, bf16[1,128,1536]{2,1,0:T(8,128)(2,1)}, ...) | async-done | bytes 786448 | tf_op jit(solution)/shard_map/psum | solution.py:281
  367.7 2.0 convert_element_type.339
  (260 shorter events, 76.8 us)
Async XLA Ops:
  7.2 90.8 %copy-start = (bf16[1,2,8,16,512]{4,3,2,1,0:T(8,128)(2,1)S(1)}, bf16[1,2,8,16,512]{4,3,2,1,0:T(8,128)(2,1)}, u32[]{:S(2)}) copy-start(bf16[1,2,8,16,512]{4,3,2,1,0:T(8,128)(2,1)} %param.7) | copy-start | bytes 786436
  7.2 64.7 %copy-start.35 = (s32[1,2,8,16]{3,2,1,0:T(8,128)S(1)}, s32[1,2,8,16]{3,2,1,0:T(8,128)}, u32[]{:S(2)}) copy-start(s32[1,2,8,16]{3,2,1,0:T(8,128)} %param.8) | copy-start | bytes 3076
  7.2 70.6 %copy-start.33 = (bf16[1,128,512]{2,1,0:T(8,128)(2,1)S(1)}, bf16[1,128,512]{2,1,0:T(8,128)(2,1)}, u32[]{:S(2)}) copy-start(bf16[1,128,512]{2,1,0:T(8,128)(2,1)} %param.11) | copy-start | bytes 393220
  7.2 31.9 %all-gather.7.cloned.1.call-start = ((), (), s32[]{:S(2)}) async-start(), calls=%async_computation.11 | async-start | bytes 1310720 | tf_op jit(solution)/shard_map/all_gather | solution.py:158
  7.9 80.5 %copy-start.44 = (bf16[1,128]{1,0:T(2,128)(2,1)S(1)}, bf16[1,128]{1,0:T(2,128)(2,1)}, u32[]{:S(2)}) copy-start(bf16[1,128]{1,0:T(2,128)(2,1)} %param.12) | copy-start | bytes 772
  7.9 63.9 %all-gather.11.cloned.1.call-start = ((), (), s32[]{:S(2)}) async-start(), calls=%async_computation.13 | async-start | bytes 1966080 | tf_op jit(solution)/shard_map/all_gather | solution.py:159
  8.7 89.3 %copy-start.28 = (bf16[1,2,8,16,512]{4,3,2,1,0:T(8,128)(2,1)S(1)}, bf16[1,2,8,16,512]{4,3,2,1,0:T(8,128)(2,1)}, u32[]{:S(2)}) copy-start(bf16[1,2,8,16,512]{4,3,2,1,0:T(8,128)(2,1)} %param.13) | copy-start | bytes 786436
  8.7 89.8 %all-gather.9.cloned.1.call-start = ((), (), s32[]{:S(2)}) async-start(), calls=%async_computation.12 | async-start | bytes 3145728 | tf_op jit(solution)/shard_map/all_gather | solution.py:174
  39.1 61.2 %all-gather.13.cloned.1.call-start = ((), (), s32[]{:S(2)}) async-start(), calls=%async_computation.14 | async-start | bytes 4718592 | tf_op jit(solution)/shard_map/all_gather | solution.py:175
  71.8 38.5 %all-gather.15.cloned.1.call-start = ((), (), s32[]{:S(2)}) async-start(), calls=%async_computation.15 | async-start | bytes 1572864 | tf_op jit(solution)/shard_map/all_gather | solution.py:176
  71.9 26.2 %collective-permute-start.3 = (s32[2,4,16]{2,1,0:T(4,128)S(1)}, s32[2,4,16]{2,1,0:T(4,128)S(1)}, u32[]{:S(2)}, u32[]{:S(2)}) collective-permute-start(s32[2,4,16]{2,1,0:T(4,128)S(1)} %get-tuple-element.46), channel_id=1, source_target_pairs={{1,0},{2,1},{3,2},{5,4},{6,5},{7,6},{9,8},{10,9},{11,10},{13,12},{... | collective-permute-start | bytes 1544 | tf_op jit(solution)/shard_map/ppermute | solution.py:23
  73.2 24.9 %collective-permute-start.2 = (s32[2,4,16]{2,1,0:T(4,128)S(1)}, s32[2,4,16]{2,1,0:T(4,128)S(1)}, u32[]{:S(2)}, u32[]{:S(2)}) collective-permute-start(s32[2,4,16]{2,1,0:T(4,128)S(1)} %get-tuple-element.47), channel_id=1, source_target_pairs={{0,1},{1,2},{2,3},{4,5},{5,6},{6,7},{8,9},{9,10},{10,11},{12,13},{... | collective-permute-start | bytes 1544 | tf_op jit(solution)/shard_map/ppermute | solution.py:22
  98.5 16.0 %copy-start.25 = (pred[128,256]{1,0:T(8,128)(4,1)}, pred[128,256]{1,0:T(8,128)(4,1)S(1)}, u32[]{:S(2)}) copy-start(pred[128,256]{1,0:T(8,128)(4,1)S(1)} %or_and_fusion) | copy-start | bytes 98308
  100.1 17.2 %copy-start.6 = (f32[8,16,512]{2,1,0:T(8,128)}, f32[8,16,512]{2,1,0:T(8,128)S(1)}, u32[]{:S(2)}) copy-start(f32[8,16,512]{2,1,0:T(8,128)S(1)} %get-tuple-element.53) | copy-start | bytes 786436
  102.3 10.2 %collective-permute-start = (bf16[4,16,1024]{2,1,0:T(8,128)(2,1)S(1)}, bf16[4,16,1024]{2,1,0:T(8,128)(2,1)S(1)}, u32[]{:S(2)}, u32[]{:S(2)}) collective-permute-start(bf16[4,16,1024]{2,1,0:T(8,128)(2,1)S(1)} %get-tuple-element.35), channel_id=1, source_target_pairs={{0,1},{1,2},{2,3},{4,5},{5,6},{6,7},{8,9},{9,10},{10,11},{12,13},{... | collective-permute-start | bytes 393224 | tf_op jit(solution)/shard_map/ppermute | solution.py:22
  105.7 7.2 %collective-permute-start.1 = (bf16[4,16,1024]{2,1,0:T(8,128)(2,1)S(1)}, bf16[4,16,1024]{2,1,0:T(8,128)(2,1)S(1)}, u32[]{:S(2)}, u32[]{:S(2)}) collective-permute-start(bf16[4,16,1024]{2,1,0:T(8,128)(2,1)S(1)} %get-tuple-element.36), channel_id=1, source_target_pairs={{1,0},{2,1},{3,2},{5,4},{6,5},{7,6},{9,8},{10,9},{11,10},{13,12},{... | collective-permute-start | bytes 393224 | tf_op jit(solution)/shard_map/ppermute | solution.py:23
  125.8 6.9 %collective-permute-start.4 = (bf16[4,16,1024]{2,1,0:T(8,128)(2,1)}, bf16[4,16,1024]{2,1,0:T(8,128)(2,1)S(1)}, u32[]{:S(2)}, u32[]{:S(2)}) collective-permute-start(bf16[4,16,1024]{2,1,0:T(8,128)(2,1)} %get-tuple-element.33), channel_id=1, source_target_pairs={{0,1},{1,2},{2,3},{4,5},{5,6},{6,7},{8,9},{9,10},{10,11},{12,13},{... | collective-permute-start | bytes 393224 | tf_op jit(solution)/shard_map/ppermute | solution.py:22
  129.2 7.3 %collective-permute-start.5 = (bf16[4,16,1024]{2,1,0:T(8,128)(2,1)S(1)}, bf16[4,16,1024]{2,1,0:T(8,128)(2,1)S(1)}, u32[]{:S(2)}, u32[]{:S(2)}) collective-permute-start(bf16[4,16,1024]{2,1,0:T(8,128)(2,1)S(1)} %get-tuple-element.34), channel_id=1, source_target_pairs={{1,0},{2,1},{3,2},{5,4},{6,5},{7,6},{9,8},{10,9},{11,10},{13,12},{... | collective-permute-start | bytes 393224 | tf_op jit(solution)/shard_map/ppermute | solution.py:23
  149.3 46.7 %all-to-all-start.5 = ((bf16[2,1,8,16,512]{4,3,2,1,0:T(8,128)(2,1)}), bf16[2,1,8,16,512]{4,3,2,1,0:T(8,128)(2,1)}, u32[]{:S(2)}, u32[]{:S(2)}) async-start(bf16[2,1,8,16,512]{4,3,2,1,0:T(8,128)(2,1)} %pad_maximum_fusion.13), calls=%async_computation.7 | async-start | bytes 524288 | tf_op jit(solution)/shard_map/all_to_all | solution.py:241
  153.4 76.8 %reduce-scatter.11.cloned.1.call-start = ((), (), s32[]{:S(2)}) async-start(), calls=%async_computation.18 | async-start | bytes 655360 | tf_op jit(solution)/shard_map/reduce_scatter | solution.py:273
  161.1 6.7 %collective-permute-start.6 = (bf16[4,16,1024]{2,1,0:T(8,128)(2,1)S(1)}, bf16[4,16,1024]{2,1,0:T(8,128)(2,1)S(1)}, u32[]{:S(2)}, u32[]{:S(2)}) collective-permute-start(bf16[4,16,1024]{2,1,0:T(8,128)(2,1)S(1)} %get-tuple-element.29), channel_id=1, source_target_pairs={{0,1},{1,2},{2,3},{4,5},{5,6},{6,7},{8,9},{9,10},{10,11},{12,13},{... | collective-permute-start | bytes 393224 | tf_op jit(solution)/shard_map/ppermute | solution.py:22
  164.4 7.5 %collective-permute-start.7 = (bf16[4,16,1024]{2,1,0:T(8,128)(2,1)S(1)}, bf16[4,16,1024]{2,1,0:T(8,128)(2,1)S(1)}, u32[]{:S(2)}, u32[]{:S(2)}) collective-permute-start(bf16[4,16,1024]{2,1,0:T(8,128)(2,1)S(1)} %get-tuple-element.30), channel_id=1, source_target_pairs={{1,0},{2,1},{3,2},{5,4},{6,5},{7,6},{9,8},{10,9},{11,10},{13,12},{... | collective-permute-start | bytes 393224 | tf_op jit(solution)/shard_map/ppermute | solution.py:23
  183.2 5.9 %collective-permute-start.8 = (bf16[4,16,1024]{2,1,0:T(8,128)(2,1)S(1)}, bf16[4,16,1024]{2,1,0:T(8,128)(2,1)S(1)}, u32[]{:S(2)}, u32[]{:S(2)}) collective-permute-start(bf16[4,16,1024]{2,1,0:T(8,128)(2,1)S(1)} %get-tuple-element.23), channel_id=1, source_target_pairs={{0,1},{1,2},{2,3},{4,5},{5,6},{6,7},{8,9},{9,10},{10,11},{12,13},{... | collective-permute-start | bytes 393224 | tf_op jit(solution)/shard_map/ppermute | solution.py:22
  186.6 6.9 %collective-permute-start.9 = (bf16[4,16,1024]{2,1,0:T(8,128)(2,1)S(1)}, bf16[4,16,1024]{2,1,0:T(8,128)(2,1)S(1)}, u32[]{:S(2)}, u32[]{:S(2)}) collective-permute-start(bf16[4,16,1024]{2,1,0:T(8,128)(2,1)S(1)} %get-tuple-element.24), channel_id=1, source_target_pairs={{1,0},{2,1},{3,2},{5,4},{6,5},{7,6},{9,8},{10,9},{11,10},{13,12},{... | collective-permute-start | bytes 393224 | tf_op jit(solution)/shard_map/ppermute | solution.py:23
  203.0 5.2 %all-to-all-start.1 = ((bf16[2,1,8,16,1024]{4,3,2,1,0:T(8,128)(2,1)}), bf16[2,1,8,16,1024]{4,3,2,1,0:T(8,128)(2,1)S(1)}, u32[]{:S(2)}, u32[]{:S(2)}) async-start(bf16[2,1,8,16,1024]{4,3,2,1,0:T(8,128)(2,1)} %pad_maximum_fusion.1), calls=%async_computation.1 | async-start | bytes 1048576 | tf_op jit(solution)/shard_map/all_to_all | solution.py:237
  206.5 49.9 %reduce-scatter.7.cloned.1.call-start = ((), (), s32[]{:S(2)}) async-start(), calls=%async_computation.16 | async-start | bytes 1310720 | tf_op jit(solution)/shard_map/reduce_scatter | solution.py:267
  214.4 5.0 %all-to-all-start.3 = ((bf16[2,1,8,16,512]{4,3,2,1,0:T(8,128)(2,1)}), bf16[2,1,8,16,512]{4,3,2,1,0:T(8,128)(2,1)S(1)}, u32[]{:S(2)}, u32[]{:S(2)}) async-start(bf16[2,1,8,16,512]{4,3,2,1,0:T(8,128)(2,1)} %pad_maximum_fusion.12), calls=%async_computation.4 | async-start | bytes 524288 | tf_op jit(solution)/shard_map/all_to_all | solution.py:239
  217.8 72.7 %reduce-scatter.9.cloned.1.call-start = ((), (), s32[]{:S(2)}) async-start(), calls=%async_computation.17 | async-start | bytes 1966080 | tf_op jit(solution)/shard_map/reduce_scatter | solution.py:270
  227.3 90.7 %reduce-scatter.13.cloned.1.call-start = ((), (), s32[]{:S(2)}) async-start(), calls=%async_computation.19 | async-start | bytes 163840
  228.8 61.8 %copy-start.3 = (bf16[1,128,8,64]{3,2,1,0:T(8,128)(2,1)S(1)}, bf16[1,128,8,64]{3,2,1,0:T(8,128)(2,1)}, u32[]{:S(2)}) copy-start(bf16[1,128,8,64]{3,2,1,0:T(8,128)(2,1)} %copy-done.2) | copy-start | bytes 393220
  228.8 62.0 %copy-start.12 = (bf16[2,512,512]{2,1,0:T(8,128)(2,1)S(1)}, bf16[2,512,512]{2,1,0:T(8,128)(2,1)}, u32[]{:S(2)}) copy-start(bf16[2,512,512]{2,1,0:T(8,128)(2,1)} %all-gather.15.cloned.1.call-done) | copy-start | bytes 3145732
  230.2 134.1 %all-reduce.11.cloned.1.call-start = ((), (), s32[]{:S(2)}) async-start(), calls=%async_computation.20 | async-start | bytes 1572864 | tf_op jit(solution)/shard_map/psum | solution.py:281
  (38 other events, 165.0 us)
Sparse Core Ops, SparseCore 0:
  9.9 29.2 all-gather.6
  40.9 30.8 all-gather.10
  73.4 10.5 all-gather.8
  85.4 13.2 all-gather.12
  100.1 10.1 all-gather.14
  202.2 23.2 reduce-scatter.10
  228.3 27.9 reduce-scatter.6
  259.3 31.1 reduce-scatter.8
  293.8 24.1 reduce-scatter.12
  320.4 43.7 all-reduce.10
where the time goes:
time: 379 us; the launch traced here: 377 us
  waiting for transfers between devices  203 us (54%)
  blocking collectives  47.4 us (13%)
  starting transfers between devices  36.4 us (10%)
  matrix products  32 us (8%)
  local copies, waits for them, and re-layouts  23.7 us (6%)
  other arithmetic  18.8 us (5%)
  between operations  15.6 us (4%)
    reduce_scatter x1, waiting for transfers between devices, body(): lax.psum_scatter(grad_sums[1][None].astype(jnp.bfloat16), 'dp', scatter_d...  34.2 us
    psum x1, waiting for transfers between devices, body(): lax.psum(merge_part_sum.astype(jnp.bfloat16), 'band').astype(jnp.float32)  33.2 us
    all_gather x1, waiting for transfers between devices, body(): lax.all_gather(qkv_weight, 'dp', axis=1, tiled=True)  32.6 us
    all_gather x1, waiting for transfers between devices, body(): lax.all_gather(merge_weight, 'dp', axis=1, tiled=True)  30.4 us
    reduce_scatter x1, waiting for transfers between devices, body(): lax.psum_scatter(grad_sums[0][None].astype(jnp.bfloat16), 'dp', scatter_d...  26.1 us
    unnamed x11, waiting for transfers between devices  24.5 us
    ppermute x5, starting transfers between devices, padded(): before = lax.ppermute(last, axis, up)  18.1 us
    ppermute x5, waiting for transfers between devices, padded(): after = lax.ppermute(first, axis, down)  12.6 us
  transfers between devices with their start and end apart: 23, of which 16 were waited for; matrix products, arithmetic and copies ran while one was open for 10% of the time, Pallas kernels for 0%

commit v1 on v0

--- a/solution.py
+++ b/solution.py
@@ -10,6 +10,28 @@
 SW = 8
 EPSILON = 1e-05
 MASKED = -1e30
+
+
+def joined_along(parts, dim):
+    parts = jnp.moveaxis(parts, 0, dim)
+    shape = parts.shape
+    return parts.reshape(*shape[:dim], shape[dim] * shape[dim + 1], *shape[dim + 2 :])
+
+
+def collected_by_bits(x, axis):
+    size = lax.axis_size(axis)
+    parts = x[None]
+    for level in range(size.bit_length() - 1):
+        bit = 1 << level
+        other = lax.ppermute(parts, axis, [(i, i ^ bit) for i in range(size)])
+        both = jnp.stack([parts, other])
+        upper = lax.axis_index(axis) >> level & 1
+        parts = jnp.where(upper == 0, both, both[::-1]).reshape(-1, *x.shape)
+    return parts
+
+
+def doubled_up(array, axis, dim):
+    return joined_along(collected_by_bits(array, axis), dim)
 
 
 def padded(shard, sides, width):
@@ -155,7 +177,7 @@
 
 def body(fields, cell_mask, merge_weight, qkv_weight, out_weight, norm_gain, out_cotangent):
     merge_rows, qkv_rows, out_rows, gain_rows = (
-        lax.all_gather(merge_weight, "dp", axis=1, tiled=True),
+        doubled_up(merge_weight, "dp", 1),
         lax.all_gather(qkv_weight, "dp", axis=1, tiled=True),
         lax.all_gather(out_weight, "dp", axis=1, tiled=True),
         lax.all_gather(norm_gain, "dp", axis=1, tiled=True),

time: 379 us -> 354 us (0.934)
  waiting for transfers between devices: 203 us -> 172 us
  starting transfers between devices: 36.4 us -> 41.4 us
    all_gather x1 -> x0, waiting for transfers between devices: 30.4 us -> none  [body(): lax.all_gather(merge_weight, 'dp', axis=1, tiled=True)]
    all_gather x1, waiting for transfers between devices: 32.6 us -> 10.3 us  [body(): lax.all_gather(qkv_weight, 'dp', axis=1, tiled=True)]
    ppermute x0 -> x2, waiting for transfers between devices: none -> 22 us  [collected_by_bits(): other = lax.ppermute(parts, axis, [(i, i ^ bit) for i in range(size)])]
    ppermute x0 -> x2, starting transfers between devices: none -> 4.87 us  [collected_by_bits(): other = lax.ppermute(parts, axis, [(i, i ^ bit) for i in range(size)])]
    unnamed x11 -> x10, waiting for transfers between devices: 24.5 us -> 23.9 us
  transfers between devices with their start and end apart: 23 -> 24, of which waited for: 16 -> 17; matrix products, arithmetic and copies ran while one was open for 10% -> 12% of each run, Pallas kernels for 0% -> 0%
where the time goes in v1:
time: 354 us; the launch traced here: 353 us
  waiting for transfers between devices  172 us (49%)
  blocking collectives  47.4 us (13%)
  starting transfers between devices  41.4 us (12%)
  matrix products  32 us (9%)
  local copies, waits for them, and re-layouts  23.7 us (7%)
  other arithmetic  21.2 us (6%)
  between operations  15.3 us (4%)
    reduce_scatter x1, waiting for transfers between devices, body(): lax.psum_scatter(grad_sums[1][None].astype(jnp.bfloat16), 'dp', scatter_d...  34.1 us
    psum x1, waiting for transfers between devices, body(): lax.psum(merge_part_sum.astype(jnp.bfloat16), 'band').astype(jnp.float32)  33.4 us
    reduce_scatter x1, waiting for transfers between devices, body(): lax.psum_scatter(grad_sums[0][None].astype(jnp.bfloat16), 'dp', scatter_d...  25.9 us
    unnamed x10, waiting for transfers between devices  23.9 us
    ppermute x2, waiting for transfers between devices, collected_by_bits(): other = lax.ppermute(parts, axis, [(i, i ^ bit) for i in range(size)])  22 us
    ppermute x5, starting transfers between devices, padded(): before = lax.ppermute(last, axis, up)  18.2 us
    ppermute x5, waiting for transfers between devices, padded(): after = lax.ppermute(first, axis, down)  12.5 us
    psum x1, blocking collectives, body(): lax.psum(gain_part_sum.astype(jnp.bfloat16), 'band').astype(jnp.float32)  11.7 us
  transfers between devices with their start and end apart: 24, of which 17 were waited for; matrix products, arithmetic and copies ran while one was open for 12% of the time, Pallas kernels for 0%

profile of v1, /device:TPU:0, one launch (start us, length us, event | category | flops | bytes accessed | tf_op | source)
XLA Modules:
  0.0 352.9 jit_solution(750922988344615636)
XLA Ops:
  8.0 3.0 collective-permute-start
  11.0 6.5 %collective-permute-done = bf16[1,1,256,512]{3,2,1,0:T(8,128)(2,1)S(1)} collective-permute-done((bf16[1,1,256,512]{3,2,1,0:T(8,128)(2,1)}, bf16[1,1,256,512]{3,2,1,0:T(8,128)(2,1)S(1)}, u32[]{:S(2)}, u32[]{:S(2)}) %collective-permute-start) | collective-permute-done | bytes 262176 | tf_op jit(solution)/shard_map/ppermute | solution.py:26
  20.5 15.5 %collective-permute-done.1 = bf16[2,1,256,512]{3,2,0,1:T(8,128)(2,1)S(1)} collective-permute-done((bf16[2,1,256,512]{3,2,0,1:T(8,128)(2,1)S(1)}, bf16[2,1,256,512]{3,2,0,1:T(8,128)(2,1)S(1)}, u32[]{:S(2)}, u32[]{:S(2)}) %collective-permute-start.1) | collective-permute-done | bytes 524320 | tf_op jit(solution)/shard_map/ppermute | solution.py:26
  37.5 10.3 %all-gather.8.cloned.1.call-done = bf16[1,512,1536]{2,1,0:T(8,128)(2,1)} async-done(((bf16[1,128,1536]{2,1,0:T(8,128)(2,1)}), bf16[1,512,1536]{2,1,0:T(8,128)(2,1)}) %all-gather.8.cloned.1.call-update) | async-done | bytes 1572880 | tf_op jit(solution)/shard_map/all_gather | solution.py:181
  49.1 4.5 %collective-permute-start.4 = (s32[2,4,16]{2,1,0:T(4,128)S(1)}, s32[2,4,16]{2,1,0:T(4,128)S(1)}, u32[]{:S(2)}, u32[]{:S(2)}) collective-permute-start(s32[2,4,16]{2,1,0:T(4,128)S(1)} %get-tuple-element.49), channel_id=1, source_target_pairs={{0,1},{1,2},{2,3},{4,5},{5,6},{6,7},{8,9},{9,10},{10,11},{12,13},{... | collective-permute-start | bytes 1544 | tf_op jit(solution)/shard_map/ppermute | solution.py:44
  53.7 10.6 %all_gather.26 = bf16[1,512,512]{2,1,0:T(8,128)(2,1)} all-gather(bf16[1,128,512]{2,1,0:T(8,128)(2,1)S(1)} %copy-done.33), channel_id=1, replica_groups=mesh['dp'=4,'segment'=2,'band'=4] {'dp'}, dimensions={1}, use_global_device_ids=true | all-gather | bytes 655360 | tf_op jit(solution)/shard_map/all_gather | solution.py:182
  64.4 7.1 %all_gather.22 = bf16[1,512]{1,0:T(2,128)(2,1)S(1)} all-gather(bf16[1,128]{1,0:T(2,128)(2,1)S(1)} %copy-done.44), channel_id=1, replica_groups=mesh['dp'=4,'segment'=2,'band'=4] {'dp'}, dimensions={1}, use_global_device_ids=true | all-gather | bytes 1280 | tf_op jit(solution)/shard_map/all_gather | solution.py:183
  78.2 3.4 collective-permute-start.2
  82.9 3.5 all-gather.12.cloned.1.call-done
  101.7 3.5 collective-permute-start.6
  108.7 3.8 %collective-permute-done.7 = bf16[4,16,1024]{2,1,0:T(8,128)(2,1)S(1)} collective-permute-done((bf16[4,16,1024]{2,1,0:T(8,128)(2,1)S(1)}, bf16[4,16,1024]{2,1,0:T(8,128)(2,1)S(1)}, u32[]{:S(2)}, u32[]{:S(2)}) %collective-permute-start.7) | collective-permute-done | bytes 131104 | tf_op jit(solution)/shard_map/ppermute | solution.py:45
  125.4 4.1 %all-to-all-start.5 = ((bf16[2,1,8,16,512]{4,3,2,1,0:T(8,128)(2,1)}), bf16[2,1,8,16,512]{4,3,2,1,0:T(8,128)(2,1)}, u32[]{:S(2)}, u32[]{:S(2)}) async-start(bf16[2,1,8,16,512]{4,3,2,1,0:T(8,128)(2,1)} %pad_maximum_fusion.15), calls=%async_computation.7 | async-start | bytes 524288 | tf_op jit(solution)/shard_map/all_to_all | solution.py:263
  137.1 3.4 collective-permute-start.8
  143.9 4.1 %collective-permute-done.9 = bf16[4,16,1024]{2,1,0:T(8,128)(2,1)S(1)} collective-permute-done((bf16[4,16,1024]{2,1,0:T(8,128)(2,1)S(1)}, bf16[4,16,1024]{2,1,0:T(8,128)(2,1)S(1)}, u32[]{:S(2)}, u32[]{:S(2)}) %collective-permute-start.9) | collective-permute-done | bytes 131104 | tf_op jit(solution)/shard_map/ppermute | solution.py:45
  148.1 2.3 fusion.127
  159.3 3.4 collective-permute-start.10
  165.1 4.4 %collective-permute-done.11 = bf16[4,16,1024]{2,1,0:T(8,128)(2,1)S(1)} collective-permute-done((bf16[4,16,1024]{2,1,0:T(8,128)(2,1)S(1)}, bf16[4,16,1024]{2,1,0:T(8,128)(2,1)S(1)}, u32[]{:S(2)}, u32[]{:S(2)}) %collective-permute-start.11) | collective-permute-done | bytes 131104 | tf_op jit(solution)/shard_map/ppermute | solution.py:45
  169.6 2.2 fusion.126
  172.0 3.9 %all_to_all.28 = bf16[2,1,8,16,512]{4,3,2,1,0:T(8,128)(2,1)S(1)} all-to-all(bf16[2,1,8,16,512]{4,3,2,1,0:T(8,128)(2,1)S(1)} %pad_maximum_fusion.16), channel_id=1, replica_groups=mesh['dp'=4,'segment'=2,'band'=4] {'segment'}, dimensions={0} | all-to-all | bytes 524288 | tf_op jit(solution)/shard_map/all_to_all | solution.py:264
  176.0 2.1 fusion.10
  179.0 3.5 all-to-all-start.1
  184.3 3.9 %all_to_all.29 = bf16[2,1,8,16,512]{4,3,2,1,0:T(8,128)(2,1)S(1)} all-to-all(bf16[2,1,8,16,512]{4,3,2,1,0:T(8,128)(2,1)S(1)} %pad_maximum_fusion.13), channel_id=1, replica_groups=mesh['dp'=4,'segment'=2,'band'=4] {'segment'}, dimensions={0} | all-to-all | bytes 524288 | tf_op jit(solution)/shard_map/all_to_all | solution.py:260
  190.5 3.4 all-to-all-start.3
  196.2 4.4 %all_to_all.30 = bf16[2,1,8,16,1536]{4,3,2,1,0:T(8,128)(2,1)S(1)} all-to-all(bf16[2,1,8,16,1536]{4,3,2,1,0:T(8,128)(2,1)S(1)} %pad_maximum_fusion.1), channel_id=1, replica_groups=mesh['dp'=4,'segment'=2,'band'=4] {'segment'}, dimensions={0} | all-to-all | bytes 1572864 | tf_op jit(solution)/shard_map/all_to_all | solution.py:262
  200.5 2.8 fusion.1
  206.3 25.9 %reduce-scatter.7.cloned.1.call-done = bf16[1,256,512]{2,1,0:T(8,128)(2,1)} async-done(((bf16[1,1024,512]{2,1,0:T(8,128)(2,1)}), bf16[1,256,512]{2,1,0:T(8,128)(2,1)}) %reduce-scatter.7.cloned.1.call-update) | async-done | bytes 262160 | tf_op jit(solution)/shard_map/reduce_scatter | solution.py:289
  232.3 34.1 %reduce-scatter.9.cloned.1.call-done = bf16[1,128,1536]{2,1,0:T(8,128)(2,1)} async-done(((bf16[1,512,1536]{2,1,0:T(8,128)(2,1)}), bf16[1,128,1536]{2,1,0:T(8,128)(2,1)}) %reduce-scatter.9.cloned.1.call-update) | async-done | bytes 393232 | tf_op jit(solution)/shard_map/reduce_scatter | solution.py:292
  266.9 3.9 %all_to_all.31 = bf16[2,1,8,16,512]{4,3,2,1,0:T(8,128)(2,1)S(1)} all-to-all(bf16[2,1,8,16,512]{4,3,2,1,0:T(8,128)(2,1)S(1)} %pad_maximum_fusion.12), channel_id=1, replica_groups=mesh['dp'=4,'segment'=2,'band'=4] {'segment'}, dimensions={0} | all-to-all | bytes 524288 | tf_op jit(solution)/shard_map/all_to_all | solution.py:258
  270.9 23.0 %reduce-scatter.13.cloned.1.call-done = bf16[128,1]{1,0:T(8,128)(2,1)} async-done(((bf16[512,1]{1,0:T(8,128)(2,1)}), bf16[128,1]{1,0:T(8,128)(2,1)}) %reduce-scatter.13.cloned.1.call-update) | async-done | bytes 272
  294.7 11.7 %psum.31 = bf16[1,128]{1,0:T(2,128)(2,1)S(1)} all-reduce(bf16[1,128]{1,0:T(2,128)(2,1)S(1)} %copy.77), channel_id=1, replica_groups=mesh['dp'=4,'segment'=2,'band'=4] {'band'}, use_global_device_ids=true, to_apply=%region_28.29 | all-reduce | flops 128 | bytes 512 | tf_op jit(solution)/shard_map/psum | solution.py:306
  306.9 33.4 %all-reduce.11.cloned.1.call-done = (bf16[1,256,512]{2,1,0:T(8,128)(2,1)}, bf16[1,128,1536]{2,1,0:T(8,128)(2,1)}, bf16[1,128,512]{2,1,0:T(8,128)(2,1)}) async-done(((bf16[1,256,512]{2,1,0:T(8,128)(2,1)}, bf16[1,128,1536]{2,1,0:T(8,128)(2,1)}, bf16[1,128,512]{2,1,0:T(8,128)(2,1)}), (bf16[1,256,512]{2,1,0:T(8,128)(2,1)}, bf16[1,128,1536]{2,1,0:T(8,128)(2,1)}, ...) | async-done | bytes 786448 | tf_op jit(solution)/shard_map/psum | solution.py:303
  343.7 2.0 convert_element_type.339
  (265 shorter events, 83.9 us)
Async XLA Ops:
  7.2 66.7 %copy-start = (bf16[1,2,8,16,512]{4,3,2,1,0:T(8,128)(2,1)S(1)}, bf16[1,2,8,16,512]{4,3,2,1,0:T(8,128)(2,1)}, u32[]{:S(2)}) copy-start(bf16[1,2,8,16,512]{4,3,2,1,0:T(8,128)(2,1)} %param.7) | copy-start | bytes 786436
  7.2 40.6 %all-gather.8.cloned.1.call-start = ((), (), s32[]{:S(2)}) async-start(), calls=%async_computation.12 | async-start | bytes 1966080 | tf_op jit(solution)/shard_map/all_gather | solution.py:181
  7.9 66.5 %all-gather.6.cloned.1.call-start = ((), (), s32[]{:S(2)}) async-start(), calls=%async_computation.11 | async-start | bytes 3145728 | tf_op jit(solution)/shard_map/all_gather | solution.py:196
  8.0 9.5 %collective-permute-start = (bf16[1,1,256,512]{3,2,1,0:T(8,128)(2,1)}, bf16[1,1,256,512]{3,2,1,0:T(8,128)(2,1)S(1)}, u32[]{:S(2)}, u32[]{:S(2)}) collective-permute-start(bf16[1,1,256,512]{3,2,1,0:T(8,128)(2,1)} %bitcast.262), channel_id=1, source_target_pairs={{0,8},{8,0},{16,24},{24,16},{1,9},{9,1},{17,25},{25,17},{2,10},{10... | collective-permute-start | bytes 786440 | tf_op jit(solution)/shard_map/ppermute | solution.py:26
  18.6 17.4 %collective-permute-start.1 = (bf16[2,1,256,512]{3,2,0,1:T(8,128)(2,1)S(1)}, bf16[2,1,256,512]{3,2,0,1:T(8,128)(2,1)S(1)}, u32[]{:S(2)}, u32[]{:S(2)}) collective-permute-start(bf16[2,1,256,512]{3,2,0,1:T(8,128)(2,1)S(1)} %get-tuple-element.34), channel_id=1, source_target_pairs={{0,16},{8,24},{16,0},{24,8},{1,17},{9,25},{17,1},{25,9},{2,18},{10... | collective-permute-start | bytes 1572872 | tf_op jit(solution)/shard_map/ppermute | solution.py:26
  36.1 17.6 %copy-start.33 = (bf16[1,128,512]{2,1,0:T(8,128)(2,1)S(1)}, bf16[1,128,512]{2,1,0:T(8,128)(2,1)}, u32[]{:S(2)}) copy-start(bf16[1,128,512]{2,1,0:T(8,128)(2,1)} %param.11) | copy-start | bytes 393220
  37.4 27.0 %copy-start.44 = (bf16[1,128]{1,0:T(2,128)(2,1)S(1)}, bf16[1,128]{1,0:T(2,128)(2,1)}, u32[]{:S(2)}) copy-start(bf16[1,128]{1,0:T(2,128)(2,1)} %param.12) | copy-start | bytes 772
  37.4 36.5 %copy-start.28 = (bf16[1,2,8,16,512]{4,3,2,1,0:T(8,128)(2,1)S(1)}, bf16[1,2,8,16,512]{4,3,2,1,0:T(8,128)(2,1)}, u32[]{:S(2)}) copy-start(bf16[1,2,8,16,512]{4,3,2,1,0:T(8,128)(2,1)} %param.13) | copy-start | bytes 786436
  37.4 38.9 %all-gather.10.cloned.1.call-start = ((), (), s32[]{:S(2)}) async-start(), calls=%async_computation.13 | async-start | bytes 4718592 | tf_op jit(solution)/shard_map/all_gather | solution.py:197
  47.8 38.6 %all-gather.12.cloned.1.call-start = ((), (), s32[]{:S(2)}) async-start(), calls=%async_computation.14 | async-start | bytes 1572864 | tf_op jit(solution)/shard_map/all_gather | solution.py:198
  47.8 26.2 %collective-permute-start.5 = (s32[2,4,16]{2,1,0:T(4,128)S(1)}, s32[2,4,16]{2,1,0:T(4,128)S(1)}, u32[]{:S(2)}, u32[]{:S(2)}) collective-permute-start(s32[2,4,16]{2,1,0:T(4,128)S(1)} %get-tuple-element.48), channel_id=1, source_target_pairs={{1,0},{2,1},{3,2},{5,4},{6,5},{7,6},{9,8},{10,9},{11,10},{13,12},{... | collective-permute-start | bytes 1544 | tf_op jit(solution)/shard_map/ppermute | solution.py:45
  49.1 24.9 %collective-permute-start.4 = (s32[2,4,16]{2,1,0:T(4,128)S(1)}, s32[2,4,16]{2,1,0:T(4,128)S(1)}, u32[]{:S(2)}, u32[]{:S(2)}) collective-permute-start(s32[2,4,16]{2,1,0:T(4,128)S(1)} %get-tuple-element.49), channel_id=1, source_target_pairs={{0,1},{1,2},{2,3},{4,5},{5,6},{6,7},{8,9},{9,10},{10,11},{12,13},{... | collective-permute-start | bytes 1544 | tf_op jit(solution)/shard_map/ppermute | solution.py:44
  74.4 16.1 %copy-start.25 = (pred[128,256]{1,0:T(8,128)(4,1)}, pred[128,256]{1,0:T(8,128)(4,1)S(1)}, u32[]{:S(2)}) copy-start(pred[128,256]{1,0:T(8,128)(4,1)S(1)} %or_and_fusion) | copy-start | bytes 98308
  76.1 17.2 %copy-start.6 = (f32[8,16,512]{2,1,0:T(8,128)}, f32[8,16,512]{2,1,0:T(8,128)S(1)}, u32[]{:S(2)}) copy-start(f32[8,16,512]{2,1,0:T(8,128)S(1)} %get-tuple-element.55) | copy-start | bytes 786436
  78.2 10.4 %collective-permute-start.2 = (bf16[4,16,1024]{2,1,0:T(8,128)(2,1)S(1)}, bf16[4,16,1024]{2,1,0:T(8,128)(2,1)S(1)}, u32[]{:S(2)}, u32[]{:S(2)}) collective-permute-start(bf16[4,16,1024]{2,1,0:T(8,128)(2,1)S(1)} %get-tuple-element.37), channel_id=1, source_target_pairs={{0,1},{1,2},{2,3},{4,5},{5,6},{6,7},{8,9},{9,10},{10,11},{12,13},{... | collective-permute-start | bytes 393224 | tf_op jit(solution)/shard_map/ppermute | solution.py:44
  81.6 7.2 %collective-permute-start.3 = (bf16[4,16,1024]{2,1,0:T(8,128)(2,1)S(1)}, bf16[4,16,1024]{2,1,0:T(8,128)(2,1)S(1)}, u32[]{:S(2)}, u32[]{:S(2)}) collective-permute-start(bf16[4,16,1024]{2,1,0:T(8,128)(2,1)S(1)} %get-tuple-element.38), channel_id=1, source_target_pairs={{1,0},{2,1},{3,2},{5,4},{6,5},{7,6},{9,8},{10,9},{11,10},{13,12},{... | collective-permute-start | bytes 393224 | tf_op jit(solution)/shard_map/ppermute | solution.py:45
  101.7 7.0 %collective-permute-start.6 = (bf16[4,16,1024]{2,1,0:T(8,128)(2,1)}, bf16[4,16,1024]{2,1,0:T(8,128)(2,1)S(1)}, u32[]{:S(2)}, u32[]{:S(2)}) collective-permute-start(bf16[4,16,1024]{2,1,0:T(8,128)(2,1)} %get-tuple-element.35), channel_id=1, source_target_pairs={{0,1},{1,2},{2,3},{4,5},{5,6},{6,7},{8,9},{9,10},{10,11},{12,13},{... | collective-permute-start | bytes 393224 | tf_op jit(solution)/shard_map/ppermute | solution.py:44
  105.2 7.3 %collective-permute-start.7 = (bf16[4,16,1024]{2,1,0:T(8,128)(2,1)S(1)}, bf16[4,16,1024]{2,1,0:T(8,128)(2,1)S(1)}, u32[]{:S(2)}, u32[]{:S(2)}) collective-permute-start(bf16[4,16,1024]{2,1,0:T(8,128)(2,1)S(1)} %get-tuple-element.36), channel_id=1, source_target_pairs={{1,0},{2,1},{3,2},{5,4},{6,5},{7,6},{9,8},{10,9},{11,10},{13,12},{... | collective-permute-start | bytes 393224 | tf_op jit(solution)/shard_map/ppermute | solution.py:45
  125.4 46.7 %all-to-all-start.5 = ((bf16[2,1,8,16,512]{4,3,2,1,0:T(8,128)(2,1)}), bf16[2,1,8,16,512]{4,3,2,1,0:T(8,128)(2,1)}, u32[]{:S(2)}, u32[]{:S(2)}) async-start(bf16[2,1,8,16,512]{4,3,2,1,0:T(8,128)(2,1)} %pad_maximum_fusion.15), calls=%async_computation.7 | async-start | bytes 524288 | tf_op jit(solution)/shard_map/all_to_all | solution.py:263
  129.5 76.8 %reduce-scatter.11.cloned.1.call-start = ((), (), s32[]{:S(2)}) async-start(), calls=%async_computation.17 | async-start | bytes 655360 | tf_op jit(solution)/shard_map/reduce_scatter | solution.py:295
  137.1 6.7 %collective-permute-start.8 = (bf16[4,16,1024]{2,1,0:T(8,128)(2,1)S(1)}, bf16[4,16,1024]{2,1,0:T(8,128)(2,1)S(1)}, u32[]{:S(2)}, u32[]{:S(2)}) collective-permute-start(bf16[4,16,1024]{2,1,0:T(8,128)(2,1)S(1)} %get-tuple-element.29), channel_id=1, source_target_pairs={{0,1},{1,2},{2,3},{4,5},{5,6},{6,7},{8,9},{9,10},{10,11},{12,13},{... | collective-permute-start | bytes 393224 | tf_op jit(solution)/shard_map/ppermute | solution.py:44
  140.5 7.5 %collective-permute-start.9 = (bf16[4,16,1024]{2,1,0:T(8,128)(2,1)S(1)}, bf16[4,16,1024]{2,1,0:T(8,128)(2,1)S(1)}, u32[]{:S(2)}, u32[]{:S(2)}) collective-permute-start(bf16[4,16,1024]{2,1,0:T(8,128)(2,1)S(1)} %get-tuple-element.30), channel_id=1, source_target_pairs={{1,0},{2,1},{3,2},{5,4},{6,5},{7,6},{9,8},{10,9},{11,10},{13,12},{... | collective-permute-start | bytes 393224 | tf_op jit(solution)/shard_map/ppermute | solution.py:45
  159.3 5.9 %collective-permute-start.10 = (bf16[4,16,1024]{2,1,0:T(8,128)(2,1)S(1)}, bf16[4,16,1024]{2,1,0:T(8,128)(2,1)S(1)}, u32[]{:S(2)}, u32[]{:S(2)}) collective-permute-start(bf16[4,16,1024]{2,1,0:T(8,128)(2,1)S(1)} %get-tuple-element.23), channel_id=1, source_target_pairs={{0,1},{1,2},{2,3},{4,5},{5,6},{6,7},{8,9},{9,10},{10,11},{12,13},{... | collective-permute-start | bytes 393224 | tf_op jit(solution)/shard_map/ppermute | solution.py:44
  162.6 6.9 %collective-permute-start.11 = (bf16[4,16,1024]{2,1,0:T(8,128)(2,1)S(1)}, bf16[4,16,1024]{2,1,0:T(8,128)(2,1)S(1)}, u32[]{:S(2)}, u32[]{:S(2)}) collective-permute-start(bf16[4,16,1024]{2,1,0:T(8,128)(2,1)S(1)} %get-tuple-element.24), channel_id=1, source_target_pairs={{1,0},{2,1},{3,2},{5,4},{6,5},{7,6},{9,8},{10,9},{11,10},{13,12},{... | collective-permute-start | bytes 393224 | tf_op jit(solution)/shard_map/ppermute | solution.py:45
  179.0 5.2 %all-to-all-start.1 = ((bf16[2,1,8,16,1024]{4,3,2,1,0:T(8,128)(2,1)}), bf16[2,1,8,16,1024]{4,3,2,1,0:T(8,128)(2,1)S(1)}, u32[]{:S(2)}, u32[]{:S(2)}) async-start(bf16[2,1,8,16,1024]{4,3,2,1,0:T(8,128)(2,1)} %pad_maximum_fusion.3), calls=%async_computation.1 | async-start | bytes 1048576 | tf_op jit(solution)/shard_map/all_to_all | solution.py:259
  182.5 49.7 %reduce-scatter.7.cloned.1.call-start = ((), (), s32[]{:S(2)}) async-start(), calls=%async_computation.15 | async-start | bytes 1310720 | tf_op jit(solution)/shard_map/reduce_scatter | solution.py:289
  190.5 5.0 %all-to-all-start.3 = ((bf16[2,1,8,16,512]{4,3,2,1,0:T(8,128)(2,1)}), bf16[2,1,8,16,512]{4,3,2,1,0:T(8,128)(2,1)S(1)}, u32[]{:S(2)}, u32[]{:S(2)}) async-start(bf16[2,1,8,16,512]{4,3,2,1,0:T(8,128)(2,1)} %pad_maximum_fusion.14), calls=%async_computation.4 | async-start | bytes 524288 | tf_op jit(solution)/shard_map/all_to_all | solution.py:261
  193.9 72.5 %reduce-scatter.9.cloned.1.call-start = ((), (), s32[]{:S(2)}) async-start(), calls=%async_computation.16 | async-start | bytes 1966080 | tf_op jit(solution)/shard_map/reduce_scatter | solution.py:292
  203.4 90.5 %reduce-scatter.13.cloned.1.call-start = ((), (), s32[]{:S(2)}) async-start(), calls=%async_computation.18 | async-start | bytes 163840
  204.8 61.6 %copy-start.3 = (bf16[1,128,8,64]{3,2,1,0:T(8,128)(2,1)S(1)}, bf16[1,128,8,64]{3,2,1,0:T(8,128)(2,1)}, u32[]{:S(2)}) copy-start(bf16[1,128,8,64]{3,2,1,0:T(8,128)(2,1)} %copy-done.2) | copy-start | bytes 393220
  204.8 61.8 %copy-start.12 = (bf16[2,512,512]{2,1,0:T(8,128)(2,1)S(1)}, bf16[2,512,512]{2,1,0:T(8,128)(2,1)}, u32[]{:S(2)}) copy-start(bf16[2,512,512]{2,1,0:T(8,128)(2,1)} %all-gather.12.cloned.1.call-done) | copy-start | bytes 3145732
  206.3 134.0 %all-reduce.11.cloned.1.call-start = ((), (), s32[]{:S(2)}) async-start(), calls=%async_computation.19 | async-start | bytes 1572864 | tf_op jit(solution)/shard_map/psum | solution.py:303
  (39 other events, 176.7 us)
Sparse Core Ops, SparseCore 0:
  9.8 37.8 all-gather.7
  49.3 10.5 all-gather.5
  61.4 13.2 all-gather.9
  76.2 10.1 all-gather.11
  178.2 23.2 reduce-scatter.10
  204.3 27.9 reduce-scatter.6
  235.2 31.0 reduce-scatter.8
  269.7 24.1 reduce-scatter.12
  296.5 43.7 all-reduce.10
